TPU v7x, 32 devices: a whole 2x2x4 slice. The times are simulated.
32 devices in a mesh: ctx: 4 (over x, core), fsdp: 8 (over z, y).
Axes of the slice: x: 2, y: 2, z: 4, core: 2. Of those that a mesh axis runs over, the one named last changes fastest.
Arguments:
- inputs: bfloat16 [2, 8, 512, 1024], P(None, 'fsdp', 'ctx'), may hold values from -6 to 6
- cotangent: bfloat16 [2, 8, 512, 1024], P(None, 'fsdp', 'ctx'), may hold values from -6 to 6
- lengths: int32 [2, 8], P(None, 'fsdp'), may hold values from 128 to 512, as said below
- query_weight: bfloat16 [1024, 1024], P('fsdp'), may hold values from -0.1875 to 0.1875
- key_weight: bfloat16 [1024, 1024], P('fsdp'), may hold values from -0.1875 to 0.1875
- value_weight: bfloat16 [1024, 1024], P('fsdp'), may hold values from -0.1875 to 0.1875
- output_weight: bfloat16 [1024, 1024], P('fsdp'), may hold values from -0.75 to 0.75
- query_bias: bfloat16 [1024], P('fsdp'), may hold values from -3 to 3
- value_bias: bfloat16 [1024], P('fsdp'), may hold values from -3 to 3
- output_bias: bfloat16 [1024], P('fsdp'), may hold values from -2 to 2
- first_gain: bfloat16 [1024], P('fsdp'), may hold values from 0.099609375 to 1.8984375
- first_shift: bfloat16 [1024], P('fsdp'), may hold values from -2 to 2
- inner_weight: bfloat16 [1024, 4096], P('fsdp'), may hold values from -0.1875 to 0.1875
- inner_bias: bfloat16 [4096], P('fsdp'), may hold values from -3 to 3
- outer_weight: bfloat16 [4096, 1024], P('fsdp'), may hold values from -0.09375 to 0.09375
- outer_bias: bfloat16 [1024], P('fsdp'), may hold values from -2 to 2
- second_gain: bfloat16 [1024], P('fsdp'), may hold values from 0.099609375 to 1.8984375
- second_shift: bfloat16 [1024], P('fsdp'), may hold values from -2 to 2
Outputs:
- layer_output: bfloat16 [2, 8, 512, 1024], P(None, 'fsdp', 'ctx')
- input_gradient: float32 [2, 8, 512, 1024], P(None, 'fsdp', 'ctx')
- query_weight_gradient: float32 [1024, 1024], P('fsdp')
- key_weight_gradient: float32 [1024, 1024], P('fsdp')
- value_weight_gradient: float32 [1024, 1024], P('fsdp')
- output_weight_gradient: float32 [1024, 1024], P('fsdp')
- query_bias_gradient: float32 [1024], P('fsdp')
- value_bias_gradient: float32 [1024], P('fsdp')
- output_bias_gradient: float32 [1024], P('fsdp')
- first_gain_gradient: float32 [1024], P('fsdp')
- first_shift_gradient: float32 [1024], P('fsdp')
- inner_weight_gradient: float32 [1024, 4096], P('fsdp')
- inner_bias_gradient: float32 [4096], P('fsdp')
- outer_weight_gradient: float32 [4096, 1024], P('fsdp')
- outer_bias_gradient: float32 [1024], P('fsdp')
- second_gain_gradient: float32 [1024], P('fsdp')
- second_shift_gradient: float32 [1024], P('fsdp')
Inputs may be any that keep to these rules, and one draw needn't show every extreme that they name: The valid slots of a sequence are its first lengths entries; in every micro-batch some sequence fills all 512 slots.
All inputs are finite; a program needn't handle non-finite values.
Results may differ from a plain program's by a relative error of at most 0.018.
Values may be sent and summed in bfloat16 or wider, within the bound.
A program may use at most 256 MiB of HBM per device.

v0:
```python
import jax
import jax.numpy as jnp
from jax import lax
from jax.sharding import PartitionSpec as P

HEAD_DIM = 64
EPSILON = 1e-06
F32 = jnp.float32
BF16 = jnp.bfloat16


def exact_gelu(hidden):
    return jax.nn.gelu(hidden, approximate=False)


def plain_product(left, right):
    return jnp.dot(left, right, preferred_element_type=F32)


def left_product(left, right):
    return lax.dot_general(left, right, (((0,), (0,)), ((), ())), preferred_element_type=F32)


def right_product(left, right):
    return lax.dot_general(left, right, (((1,), (1,)), ((), ())), preferred_element_type=F32)


def column_sums(rows):
    return jnp.sum(rows.astype(F32), axis=0)


def norm_parts(total):
    average = jnp.mean(total, axis=-1, keepdims=True)
    centered = total - average
    variance = jnp.mean(centered * centered, axis=-1, keepdims=True)
    rate = lax.rsqrt(variance + EPSILON)
    return (centered * rate, rate)


def norm_back(unit, rate, grad):
    return rate * (
        grad
        - jnp.mean(grad, axis=-1, keepdims=True)
        - unit * jnp.mean(grad * unit, axis=-1, keepdims=True)
    )


def split_columns(packed, widths):
    pieces = []
    start = 0
    for width in widths:
        pieces.append(packed[..., start : start + width])
        start += width
    return pieces


def attention_forward(queries, keys_all, values_all, key_valid, heads):
    shape = queries.shape[:2] + (heads, HEAD_DIM)
    key_shape = keys_all.shape[:2] + (heads, HEAD_DIM)
    scores = jnp.einsum(
        "sqhd,skhd->shqk",
        queries.reshape(shape),
        keys_all.reshape(key_shape),
        preferred_element_type=F32,
    ) * HEAD_DIM ** (-0.5)
    scores = jnp.where(key_valid[:, None, None, :], scores, -1e30)
    top = jnp.max(scores, axis=-1, keepdims=True)
    weights = jnp.exp(scores - top)
    probs = (weights / jnp.sum(weights, axis=-1, keepdims=True)).astype(BF16)
    context = jnp.einsum(
        "shqk,skhd->sqhd", probs, values_all.reshape(key_shape), preferred_element_type=F32
    )
    return (context.reshape(queries.shape).astype(BF16), probs)


def attention_backward(queries, keys_all, values_all, probs, context_grad, heads):
    shape = queries.shape[:2] + (heads, HEAD_DIM)
    key_shape = keys_all.shape[:2] + (heads, HEAD_DIM)
    scale = HEAD_DIM ** (-0.5)
    grad_heads = context_grad.reshape(shape)
    wide = probs.astype(F32)
    probs_grad = jnp.einsum(
        "sqhd,skhd->shqk", grad_heads, values_all.reshape(key_shape), preferred_element_type=F32
    )
    inner_total = jnp.sum(wide * probs_grad, axis=-1, keepdims=True)
    scores_grad = (wide * (probs_grad - inner_total)).astype(BF16)
    query_grad = jnp.einsum(
        "shqk,skhd->sqhd", scores_grad, keys_all.reshape(key_shape), preferred_element_type=F32
    )
    key_part = jnp.einsum(
        "shqk,sqhd->skhd", scores_grad, queries.reshape(shape), preferred_element_type=F32
    )
    value_part = jnp.einsum("shqk,sqhd->skhd", probs, grad_heads, preferred_element_type=F32)
    return (
        (query_grad * scale).astype(BF16).reshape(queries.shape),
        (key_part * scale).astype(BF16).reshape(keys_all.shape),
        value_part.astype(BF16).reshape(values_all.shape),
    )


def gather_rows(part):
    return lax.all_gather(part, "fsdp", axis=0, tiled=True)


def reduce_rows(part):
    share = lax.psum_scatter(part.astype(BF16), "fsdp", scatter_dimension=0, tiled=True)
    return lax.psum(share, "ctx").astype(F32)


def body(
    inputs,
    cotangent,
    lengths,
    query_weight,
    key_weight,
    value_weight,
    output_weight,
    query_bias,
    value_bias,
    output_bias,
    first_gain,
    first_shift,
    inner_weight,
    inner_bias,
    outer_weight,
    outer_bias,
    second_gain,
    second_shift,
):
    vectors = (
        query_bias,
        value_bias,
        output_bias,
        first_gain,
        first_shift,
        inner_bias,
        outer_bias,
        second_gain,
        second_shift,
    )
    widths = [member.shape[0] for member in vectors]
    packed = lax.all_gather(jnp.concatenate(vectors), "fsdp", axis=0, tiled=False)
    (
        bias_query,
        bias_value,
        bias_output,
        gain_first,
        shift_first,
        bias_inner,
        bias_outer,
        gain_second,
        shift_second,
    ) = [piece.reshape(-1).astype(F32) for piece in split_columns(packed, widths)]
    full_qkv = gather_rows(jnp.concatenate((query_weight, key_weight, value_weight), axis=1))
    full_output = gather_rows(output_weight)
    full_inner = gather_rows(inner_weight)
    full_outer = gather_rows(outer_weight)
    micro, seqs, block_len, width = inputs.shape
    heads = width // HEAD_DIM
    ctx_size = lax.axis_size("ctx")
    total_slots = block_len * ctx_size
    group = micro * seqs
    rows = group * block_len
    flat_len = lengths.reshape(group)
    local_pos = lax.axis_index("ctx") * block_len + jnp.arange(block_len, dtype=jnp.int32)
    row_mask = (local_pos[None, :] < flat_len[:, None]).astype(F32).reshape(rows, 1)
    key_valid = jnp.arange(total_slots, dtype=jnp.int32)[None, :] < flat_len[:, None]
    flat_rows = inputs.reshape(rows, width)
    qkv = plain_product(flat_rows, full_qkv)
    queries = (qkv[:, :width] + bias_query).astype(BF16)
    keys_values = jnp.concatenate(
        (qkv[:, width : 2 * width], qkv[:, 2 * width :] + bias_value), axis=1
    ).astype(BF16)
    keys_values_all = lax.all_gather(
        keys_values.reshape(group, block_len, 2 * width), "ctx", axis=1, tiled=True
    )
    keys_all = keys_values_all[:, :, :width]
    values_all = keys_values_all[:, :, width:]
    queries3 = queries.reshape(group, block_len, width)
    context, probs = attention_forward(queries3, keys_all, values_all, key_valid, heads)
    context = context.reshape(rows, width)
    first_sum = flat_rows.astype(F32) + plain_product(context, full_output) + bias_output
    first_unit, first_rate = norm_parts(first_sum)
    normed = first_unit * gain_first + shift_first
    normed_low = normed.astype(BF16)
    hidden = plain_product(normed_low, full_inner) + bias_inner
    active, gelu_back = jax.vjp(exact_gelu, hidden)
    active_low = active.astype(BF16)
    second_sum = normed + plain_product(active_low, full_outer) + bias_outer
    second_unit, second_rate = norm_parts(second_sum)
    output = ((second_unit * gain_second + shift_second) * row_mask).astype(BF16)
    out_grad = cotangent.reshape(rows, width).astype(F32) * row_mask
    second_gain_part = jnp.sum(out_grad * second_unit, axis=0)
    second_shift_part = jnp.sum(out_grad, axis=0)
    second_grad = norm_back(second_unit, second_rate, out_grad * gain_second)
    second_low = second_grad.astype(BF16)
    outer_weight_part = left_product(active_low, second_low).astype(BF16)
    outer_bias_part = column_sums(second_low)
    (hidden_grad,) = gelu_back(right_product(second_low, full_outer))
    hidden_low = hidden_grad.astype(BF16)
    inner_weight_part = left_product(normed_low, hidden_low).astype(BF16)
    inner_bias_part = column_sums(hidden_low)
    normed_grad = second_grad + right_product(hidden_low, full_inner)
    first_gain_part = jnp.sum(normed_grad * first_unit, axis=0)
    first_shift_part = jnp.sum(normed_grad, axis=0)
    first_grad = norm_back(first_unit, first_rate, normed_grad * gain_first)
    branch_low = first_grad.astype(BF16)
    output_weight_part = left_product(context, branch_low).astype(BF16)
    output_bias_part = column_sums(branch_low)
    context_grad = right_product(branch_low, full_output).astype(BF16)
    query_grad, key_part, value_part = attention_backward(
        queries3, keys_all, values_all, probs, context_grad.reshape(queries3.shape), heads
    )
    keys_values_grad = lax.psum_scatter(
        jnp.concatenate((key_part, value_part), axis=2), "ctx", scatter_dimension=1, tiled=True
    ).reshape(rows, 2 * width)
    qkv_grad = jnp.concatenate((query_grad.reshape(rows, width), keys_values_grad), axis=1)
    qkv_weight_part = left_product(flat_rows, qkv_grad).astype(BF16)
    query_bias_part = column_sums(qkv_grad[:, :width])
    value_bias_part = column_sums(qkv_grad[:, 2 * width :])
    input_grad = first_grad + right_product(qkv_grad, full_qkv)
    qkv_share = reduce_rows(qkv_weight_part)
    output_share = reduce_rows(output_weight_part)
    inner_share = reduce_rows(inner_weight_part)
    outer_share = reduce_rows(outer_weight_part)
    vector_parts = (
        query_bias_part,
        value_bias_part,
        output_bias_part,
        first_gain_part,
        first_shift_part,
        inner_bias_part,
        outer_bias_part,
        second_gain_part,
        second_shift_part,
    )
    fsdp_size = lax.axis_size("fsdp")
    packed_parts = jnp.concatenate([part.reshape(fsdp_size, -1) for part in vector_parts], axis=1)
    vector_share = lax.psum(
        lax.psum_scatter(packed_parts, "fsdp", scatter_dimension=0, tiled=True), "ctx"
    )[0]
    shares = split_columns(vector_share, widths)
    query_share, key_share, value_share = split_columns(qkv_share, [width] * 3)
    return (
        output.reshape(inputs.shape),
        input_grad.reshape(inputs.shape),
        query_share,
        key_share,
        value_share,
        output_share,
        shares[0],
        shares[1],
        shares[2],
        shares[3],
        shares[4],
        inner_share,
        shares[5],
        outer_share,
        shares[6],
        shares[7],
        shares[8],
    )


def solution(mesh):
    data = P(None, "fsdp", "ctx", None)
    matrix = P("fsdp", None)
    vector = P("fsdp")
    return jax.shard_map(
        body,
        mesh=mesh,
        in_specs=(data, data, P(None, "fsdp"))
        + (matrix,) * 4
        + (vector,) * 5
        + (matrix, vector, matrix, vector, vector, vector),
        out_specs=(data, data)
        + (matrix,) * 4
        + (vector,) * 5
        + (matrix, vector, matrix, vector, vector, vector),
        check_vma=False,
    )
```

profile of v0, /device:TPU:0, one launch (start us, length us, event | category | flops | bytes accessed | tf_op | source)
XLA Modules:
  0.0 1151.7 jit_solution(14489153221293311323)
XLA Ops:
  16.9 33.0 %all-gather.1 = bf16[8,1,1536]{2,1,0:T(2,128)(2,1)S(1)} all-gather(bf16[1,1,1536]{2,1,0:T(2,128)(2,1)S(1)} %reshape.321), channel_id=2, replica_groups=mesh['ctx'=4,'fsdp'=8] {'fsdp'}, dimensions={0}, use_global_device_ids=true | all-gather | bytes 27648 | tf_op jit(solution)/shard_map/all_gather | solution.py:142
  50.0 63.2 %all-gather.8.cloned.1.call-done = bf16[1024,3072]{1,0:T(8,128)(2,1)} async-done(((bf16[128,3072]{1,0:T(8,128)(2,1)}), bf16[1024,3072]{1,0:T(8,128)(2,1)}) %all-gather.8.cloned.1.call-update) | async-done | bytes 6291472 | tf_op jit(solution)/shard_map/all_gather | solution.py:102
  124.1 28.1 %all-gather.10.cloned.1.call-done = bf16[2,512,2048]{2,1,0:T(8,128)(2,1)} async-done(((bf16[2,128,2048]{2,1,0:T(8,128)(2,1)}), bf16[2,512,2048]{2,1,0:T(8,128)(2,1)}) %all-gather.10.cloned.1.call-update) | async-done | bytes 4194320 | tf_op jit(solution)/shard_map/all_gather | solution.py:174
  162.0 7.7 fusion.54
  178.5 25.1 %all-gather.12.cloned.1.call-done = bf16[1024,1024]{1,0:T(8,128)(2,1)} async-done(((bf16[128,1024]{1,0:T(8,128)(2,1)}), bf16[1024,1024]{1,0:T(8,128)(2,1)}) %all-gather.12.cloned.1.call-update) | async-done | bytes 2097168 | tf_op jit(solution)/shard_map/all_gather | solution.py:102
  206.5 122.5 %all-gather.14.cloned.1.call-done = bf16[1024,4096]{1,0:T(8,128)(2,1)} async-done(((bf16[128,4096]{1,0:T(8,128)(2,1)}), bf16[1024,4096]{1,0:T(8,128)(2,1)}) %all-gather.14.cloned.1.call-update) | async-done | bytes 8388624 | tf_op jit(solution)/shard_map/all_gather | solution.py:102
  329.0 16.2 %multiply_convert_fusion.1 = (bf16[256,4096]{1,0:T(8,128)(2,1)}, f32[256,4096]{1,0:T(8,128)}, f32[256,4096]{1,0:T(8,128)}) fusion(f32[4096]{0:T(1024)S(1)} %bitcast.181, bf16[1024,4096]{1,0:T(8,128)(2,1)} %all-gather.14.cloned.1.call-done, f32[256,1024]{1,0:T(8,128)S(1)} %get-tuple-element.115, f32[1024]{0:T(1024)S(1)} %get-tuple-element.97, ...), kind=kOutput, calls=%fused_computation.19 | convolution fusion | flops 2218000384 | bytes 19949568 | tf_op jit(solution)/shard_map/dot_general | solution.py:17
  345.3 108.9 %all-gather.16.cloned.1.call-done = bf16[4096,1024]{1,0:T(8,128)(2,1)} async-done(((bf16[512,1024]{1,0:T(8,128)(2,1)}), bf16[4096,1024]{1,0:T(8,128)(2,1)}) %all-gather.16.cloned.1.call-update) | async-done | bytes 8388624 | tf_op jit(solution)/shard_map/all_gather | solution.py:102
  454.2 6.5 fusion.56
  462.9 11.1 convert_reduce_fusion
  474.1 6.9 multiply_reduce_fusion.1
  522.4 34.0 %reduce-scatter.8.cloned.1.call-done = bf16[2,128,2048]{2,1,0:T(8,128)(2,1)} async-done(((bf16[2,512,2048]{2,1,0:T(8,128)(2,1)}), bf16[2,128,2048]{2,1,0:T(8,128)(2,1)}) %reduce-scatter.8.cloned.1.call-update) | async-done | bytes 1048592 | tf_op jit(solution)/shard_map/reduce_scatter | solution.py:214
  556.4 5.9 convert_bitcast_fusion
  562.3 8.7 copy.83
  574.6 7.3 convolution_convert_fusion.1
  583.1 7.2 convolution_convert_fusion
  591.8 97.3 %reduce-scatter.16.cloned.1.call-done = bf16[128,3072]{1,0:T(8,128)(2,1)} async-done(((bf16[1024,3072]{1,0:T(8,128)(2,1)}), bf16[128,3072]{1,0:T(8,128)(2,1)}) %reduce-scatter.16.cloned.1.call-update) | async-done | bytes 786448
  691.4 69.1 %reduce-scatter.10.cloned.1.call-done = bf16[128,1024]{1,0:T(8,128)(2,1)} async-done(((bf16[1024,1024]{1,0:T(8,128)(2,1)}), bf16[128,1024]{1,0:T(8,128)(2,1)}) %reduce-scatter.10.cloned.1.call-update) | async-done | bytes 262160 | tf_op jit(solution)/shard_map/reduce_scatter | solution.py:106
  760.5 152.1 %reduce-scatter.12.cloned.1.call-done = bf16[128,4096]{1,0:T(8,128)(2,1)} async-done(((bf16[1024,4096]{1,0:T(8,128)(2,1)}), bf16[128,4096]{1,0:T(8,128)(2,1)}) %reduce-scatter.12.cloned.1.call-update) | async-done | bytes 1048592 | tf_op jit(solution)/shard_map/reduce_scatter | solution.py:106
  912.6 151.5 %reduce-scatter.14.cloned.1.call-done = bf16[512,1024]{1,0:T(8,128)(2,1)} async-done(((bf16[4096,1024]{1,0:T(8,128)(2,1)}), bf16[512,1024]{1,0:T(8,128)(2,1)}) %reduce-scatter.14.cloned.1.call-update) | async-done | bytes 1048592 | tf_op jit(solution)/shard_map/reduce_scatter | solution.py:106
  1064.2 35.6 %all-reduce = f32[8,1536]{1,0:T(8,128)S(1)} all-reduce(f32[8,1536]{1,0:T(8,128)S(1)} %constant_dynamic-update-slice_fusion), channel_id=6, replica_groups=mesh['ctx'=4,'fsdp'=8] {'fsdp'}, use_global_device_ids=true, to_apply=%region_25.26.clone | all-reduce | flops 12288 | bytes 98304
  1100.5 5.8 psum.37
  1107.3 5.9 convolution_add_fusion.2
  1113.3 22.2 %all-reduce.4.cloned.1.call-done = (bf16[128,3072]{0,1:T(8,128)(2,1)}, bf16[128,1024]{1,0:T(8,128)(2,1)}, bf16[128,4096]{1,0:T(8,128)(2,1)}, bf16[512,1024]{1,0:T(8,128)(2,1)}) async-done(((bf16[128,3072]{0,1:T(8,128)(2,1)}, bf16[128,1024]{1,0:T(8,128)(2,1)}, bf16[128,4096]{1,0:T(8,128)(2,1)}, bf16[512,1024]{1,0:T(8,128)(2,1)}), (bf16[128,3072]{0,1:T(8,128)(2,1)}, bf16[128,1024]{1,0:T(8,128)(2,1)}, ...) | async-done | bytes 3145744 | tf_op jit(solution)/shard_map/psum | solution.py:107
  (149 shorter events, 105.2 us)
Async XLA Ops:
  7.2 105.9 %all-gather.8.cloned.1.call-start = ((), (), s32[]{:S(2)}) async-start(), calls=%async_computation.5 | async-start | bytes 7077888 | tf_op jit(solution)/shard_map/all_gather | solution.py:102
  9.3 142.8 %all-gather.10.cloned.1.call-start = ((), (), s32[]{:S(2)}) async-start(), calls=%async_computation.6 | async-start | bytes 5242880 | tf_op jit(solution)/shard_map/all_gather | solution.py:174
  118.0 3.4 copy-start.19
  118.0 3.4 copy-start.8
  119.3 84.3 %all-gather.12.cloned.1.call-start = ((), (), s32[]{:S(2)}) async-start(), calls=%async_computation.7 | async-start | bytes 2359296 | tf_op jit(solution)/shard_map/all_gather | solution.py:102
  120.1 209.0 %all-gather.14.cloned.1.call-start = ((), (), s32[]{:S(2)}) async-start(), calls=%async_computation.8 | async-start | bytes 9437184 | tf_op jit(solution)/shard_map/all_gather | solution.py:102
  120.6 333.5 %all-gather.16.cloned.1.call-start = ((), (), s32[]{:S(2)}) async-start(), calls=%async_computation.9 | async-start | bytes 9437184 | tf_op jit(solution)/shard_map/all_gather | solution.py:102
  121.2 435.2 %reduce-scatter.8.cloned.1.call-start = ((), (), s32[]{:S(2)}) async-start(), calls=%async_computation.10 | async-start | bytes 5242880 | tf_op jit(solution)/shard_map/reduce_scatter | solution.py:214
  159.1 2.9 copy-start.14
  454.2 6.8 copy-start.9
  460.7 2.2 copy-start.21
  462.8 11.2 copy-start.11
  474.0 6.9 copy-start.13
  474.0 8.3 copy-start.5
  489.5 4.0 copy-start.1
  489.5 4.0 copy-start.10
  494.2 6.2 copy-start.15
  513.6 175.6 %reduce-scatter.16.cloned.1.call-start = ((), (), s32[]{:S(2)}) async-start(), calls=%async_computation.14 | async-start | bytes 7077888
  571.0 189.6 %reduce-scatter.10.cloned.1.call-start = ((), (), s32[]{:S(2)}) async-start(), calls=%async_computation.11 | async-start | bytes 2359296 | tf_op jit(solution)/shard_map/reduce_scatter | solution.py:106
  574.3 338.3 %reduce-scatter.12.cloned.1.call-start = ((), (), s32[]{:S(2)}) async-start(), calls=%async_computation.12 | async-start | bytes 9437184 | tf_op jit(solution)/shard_map/reduce_scatter | solution.py:106
  581.9 482.2 %reduce-scatter.14.cloned.1.call-start = ((), (), s32[]{:S(2)}) async-start(), calls=%async_computation.13 | async-start | bytes 9437184 | tf_op jit(solution)/shard_map/reduce_scatter | solution.py:106
  590.3 545.2 %all-reduce.4.cloned.1.call-start = ((), (), s32[]{:S(2)}) async-start(), calls=%async_computation.15 | async-start | bytes 6291456 | tf_op jit(solution)/shard_map/psum | solution.py:107
  1135.5 7.1 copy-start.16
  1137.8 6.3 copy-start.17
  (9 other events, 12.2 us)
Sparse Core Ops, SparseCore 0:
  10.8 102.3 all-gather.7
  119.5 32.6 all-gather.9
  154.3 49.2 all-gather.11
  205.6 123.4 all-gather.13
  331.0 123.1 all-gather.15
  513.7 42.6 reduce-scatter.7
  571.1 117.9 reduce-scatter.15
  693.6 66.8 reduce-scatter.9
  764.6 147.9 reduce-scatter.11
  916.1 147.9 reduce-scatter.13
  1067.4 68.0 all-reduce.3
where the time goes:
time: 1160 us; the launch traced here: 1150 us
  waiting for transfers between devices  876 us (76%)
  matrix products  98.7 us (9%)
  blocking collectives  74.4 us (6%)
  local copies, waits for them, and re-layouts  62.8 us (5%)
  other arithmetic  24.6 us (2%)
  between operations  14.5 us (1%)
    reduce_scatter x3, waiting for transfers between devices, reduce_rows(): lax.psum_scatter(part.astype(BF16), 'fsdp', scatter_dimension=0, tiled=True)  373 us
    all_gather x4, waiting for transfers between devices, gather_rows(): return lax.all_gather(part, 'fsdp', axis=0, tiled=True)  320 us
    unnamed x12, waiting for transfers between devices  99.2 us
    unnamed x1, blocking collectives  35.6 us
    reduce_scatter x1, waiting for transfers between devices, body(): lax.psum_scatter(jnp.concatenate((key_part, value_part), axis=2), 'ctx',...  34 us
    all_gather x1, blocking collectives, body(): lax.all_gather(jnp.concatenate(vectors), 'fsdp', axis=0, tiled=False)  33 us
    unnamed x70, local copies, waits for them, and re-layouts  31.4 us
    dot_general x4, matrix products, plain_product(): return jnp.dot(left, right, preferred_element_type=F32)  30.2 us
  transfers between devices with their start and end apart: 11, of which 11 were waited for; matrix products, arithmetic and copies ran while one was open for 8% of the time, Pallas kernels for 0%

commit v1 on v0

--- a/solution.py
+++ b/solution.py
@@ -7,6 +7,27 @@
 EPSILON = 1e-06
 F32 = jnp.float32
 BF16 = jnp.bfloat16
+
+
+def joined_along(pieces, dim):
+    lengths = list(pieces.shape[1:])
+    lengths[dim] *= pieces.shape[0]
+    return jnp.moveaxis(pieces, 0, dim).reshape(lengths)
+
+
+def grow_blocks(x, axis):
+    length, here = (lax.axis_size(axis), lax.axis_index(axis))
+    tiles, bit = (x[None], 1)
+    while bit < length:
+        received = lax.ppermute(tiles, axis, [(i, i ^ bit) for i in range(length)])
+        low = here & bit == 0
+        tiles = jnp.concatenate([jnp.where(low, tiles, received), jnp.where(low, received, tiles)])
+        bit *= 2
+    return tiles
+
+
+def doubled_up(x, axis, dim):
+    return joined_along(grow_blocks(x, axis), dim)
 
 
 def exact_gelu(hidden):
@@ -171,9 +192,7 @@
     keys_values = jnp.concatenate(
         (qkv[:, width : 2 * width], qkv[:, 2 * width :] + bias_value), axis=1
     ).astype(BF16)
-    keys_values_all = lax.all_gather(
-        keys_values.reshape(group, block_len, 2 * width), "ctx", axis=1, tiled=True
-    )
+    keys_values_all = doubled_up(keys_values.reshape(group, block_len, 2 * width), "ctx", 1)
     keys_all = keys_values_all[:, :, :width]
     values_all = keys_values_all[:, :, width:]
     queries3 = queries.reshape(group, block_len, width)

time: 1160 us -> 1120 us (0.966)
  waiting for transfers between devices: 876 us -> 835 us
    all_gather x4, waiting for transfers between devices: 320 us -> 261 us  [gather_rows(): return lax.all_gather(part, 'fsdp', axis=0, tiled=True)]
    ppermute x0 -> x2, waiting for transfers between devices: none -> 44.9 us  [grow_blocks(): received = lax.ppermute(tiles, axis, [(i, i ^ bit) for i in range(length)])]
    all_gather x1 -> x0, waiting for transfers between devices: 28.1 us -> none  [body(): lax.all_gather(keys_values.reshape(group, block_len, 2 * width), 'ctx', a...]
    unnamed x70 -> x90, local copies, waits for them, and re-layouts: 31.4 us -> 25.9 us
    unnamed x12 -> x11, waiting for transfers between devices: 99.2 us -> 100 us
  transfers between devices with their start and end apart: 11 -> 12, of which waited for: 11 -> 11; matrix products, arithmetic and copies ran while one was open for 8% -> 8% of each run, Pallas kernels for 0% -> 0%
where the time goes in v1:
time: 1120 us; the launch traced here: 1110 us
  waiting for transfers between devices  835 us (75%)
  matrix products  98.8 us (9%)
  blocking collectives  74.5 us (7%)
  local copies, waits for them, and re-layouts  55.4 us (5%)
  other arithmetic  30.1 us (3%)
  between operations  15.3 us (1%)
    reduce_scatter x3, waiting for transfers between devices, reduce_rows(): lax.psum_scatter(part.astype(BF16), 'fsdp', scatter_dimension=0, tiled=True)  373 us
    all_gather x4, waiting for transfers between devices, gather_rows(): return lax.all_gather(part, 'fsdp', axis=0, tiled=True)  261 us
    unnamed x11, waiting for transfers between devices  100 us
    ppermute x2, waiting for transfers between devices, grow_blocks(): received = lax.ppermute(tiles, axis, [(i, i ^ bit) for i in range(length)])  44.9 us
    unnamed x1, blocking collectives  35.6 us
    reduce_scatter x1, waiting for transfers between devices, body(): lax.psum_scatter(jnp.concatenate((key_part, value_part), axis=2), 'ctx',...  34 us
    all_gather x1, blocking collectives, body(): lax.all_gather(jnp.concatenate(vectors), 'fsdp', axis=0, tiled=False)  32.9 us
    dot_general x4, matrix products, plain_product(): return jnp.dot(left, right, preferred_element_type=F32)  30 us
  transfers between devices with their start and end apart: 12, of which 11 were waited for; matrix products, arithmetic and copies ran while one was open for 8% of the time, Pallas kernels for 0%

profile of v1, /device:TPU:0, one launch (start us, length us, event | category | flops | bytes accessed | tf_op | source)
XLA Modules:
  0.0 1111.5 jit_solution(11913683890049771337)
XLA Ops:
  13.6 32.9 %all-gather.1 = bf16[8,1,1536]{2,1,0:T(2,128)(2,1)S(1)} all-gather(bf16[1,1,1536]{2,1,0:T(2,128)(2,1)S(1)} %reshape.351), channel_id=2, replica_groups=mesh['ctx'=4,'fsdp'=8] {'fsdp'}, dimensions={0}, use_global_device_ids=true | all-gather | bytes 27648 | tf_op jit(solution)/shard_map/all_gather | solution.py:163
  46.5 66.6 %all-gather.7.cloned.1.call-done = bf16[1024,3072]{1,0:T(8,128)(2,1)} async-done(((bf16[128,3072]{1,0:T(8,128)(2,1)}), bf16[1024,3072]{1,0:T(8,128)(2,1)}) %all-gather.7.cloned.1.call-update) | async-done | bytes 6291472 | tf_op jit(solution)/shard_map/all_gather | solution.py:123
  131.7 42.1 %collective-permute-done.1 = bf16[2,2,128,2048]{3,2,0,1:T(8,128)(2,1)} collective-permute-done((bf16[2,2,128,2048]{3,2,0,1:T(8,128)(2,1)}, bf16[2,2,128,2048]{3,2,0,1:T(8,128)(2,1)}, u32[]{:S(2)}, u32[]{:S(2)}) %collective-permute-start.1) | collective-permute-done | bytes 2097184 | tf_op jit(solution)/shard_map/ppermute | solution.py:22
  183.4 7.6 fusion.54
  202.8 85.5 %all-gather.11.cloned.1.call-done = bf16[1024,4096]{1,0:T(8,128)(2,1)} async-done(((bf16[128,4096]{1,0:T(8,128)(2,1)}), bf16[1024,4096]{1,0:T(8,128)(2,1)}) %all-gather.11.cloned.1.call-update) | async-done | bytes 8388624 | tf_op jit(solution)/shard_map/all_gather | solution.py:123
  288.3 16.2 %multiply_convert_fusion.1 = (bf16[256,4096]{1,0:T(8,128)(2,1)}, f32[256,4096]{1,0:T(8,128)}, f32[256,4096]{1,0:T(8,128)}) fusion(f32[4096]{0:T(1024)S(1)} %bitcast.191, bf16[1024,4096]{1,0:T(8,128)(2,1)} %all-gather.11.cloned.1.call-done, f32[256,1024]{1,0:T(8,128)S(1)} %get-tuple-element.119, f32[1024]{0:T(1024)S(1)} %get-tuple-element.101, ...), kind=kOutput, calls=%fused_computation.20 | convolution fusion | flops 2218000384 | bytes 19949568 | tf_op jit(solution)/shard_map/dot_general | solution.py:38
  304.5 108.9 %all-gather.13.cloned.1.call-done = bf16[4096,1024]{1,0:T(8,128)(2,1)} async-done(((bf16[512,1024]{1,0:T(8,128)(2,1)}), bf16[4096,1024]{1,0:T(8,128)(2,1)}) %all-gather.13.cloned.1.call-update) | async-done | bytes 8388624 | tf_op jit(solution)/shard_map/all_gather | solution.py:123
  413.3 6.5 fusion.56
  422.1 11.3 %convert_reduce_fusion = (f32[4096]{0:T(1024)S(1)}, bf16[256,4096]{1,0:T(8,128)(2,1)S(1)}) fusion(f32[256,4096]{1,0:T(8,128)S(1)} %copy-done.31, f32[256,4096]{1,0:T(8,128)} %get-tuple-element.120, bf16[4096,1024]{1,0:T(8,128)(2,1)} %all-gather.13.cloned.1.call-done, f32[256,1024]{1,0:T(8,128)S(1)} %get-tuple-element.81), kind=kOutput, calls=%fused_computation.17 | convolution fusion | flops 2164518912 | bytes 19939328 | tf_op jit(solution)/shard_map/dot_general | solution.py:46
  433.5 6.9 multiply_reduce_fusion.1
  467.9 4.7 pad_maximum_fusion.1
  481.4 34.0 %reduce-scatter.8.cloned.1.call-done = bf16[2,128,2048]{2,1,0:T(8,128)(2,1)} async-done(((bf16[2,512,2048]{2,1,0:T(8,128)(2,1)}), bf16[2,128,2048]{2,1,0:T(8,128)(2,1)}) %reduce-scatter.8.cloned.1.call-update) | async-done | bytes 1048592 | tf_op jit(solution)/shard_map/reduce_scatter | solution.py:233
  515.5 5.8 convert_bitcast_fusion
  521.3 8.6 copy.85
  533.4 7.5 convolution_convert_fusion
  540.9 7.3 convolution_convert_fusion.1
  549.7 98.3 %reduce-scatter.16.cloned.1.call-done = bf16[128,3072]{1,0:T(8,128)(2,1)} async-done(((bf16[1024,3072]{1,0:T(8,128)(2,1)}), bf16[128,3072]{1,0:T(8,128)(2,1)}) %reduce-scatter.16.cloned.1.call-update) | async-done | bytes 786448
  650.3 69.3 %reduce-scatter.10.cloned.1.call-done = bf16[128,1024]{1,0:T(8,128)(2,1)} async-done(((bf16[1024,1024]{1,0:T(8,128)(2,1)}), bf16[128,1024]{1,0:T(8,128)(2,1)}) %reduce-scatter.10.cloned.1.call-update) | async-done | bytes 262160 | tf_op jit(solution)/shard_map/reduce_scatter | solution.py:127
  719.6 152.1 %reduce-scatter.14.cloned.1.call-done = bf16[512,1024]{1,0:T(8,128)(2,1)} async-done(((bf16[4096,1024]{1,0:T(8,128)(2,1)}), bf16[512,1024]{1,0:T(8,128)(2,1)}) %reduce-scatter.14.cloned.1.call-update) | async-done | bytes 1048592 | tf_op jit(solution)/shard_map/reduce_scatter | solution.py:127
  871.8 151.7 %reduce-scatter.12.cloned.1.call-done = bf16[128,4096]{1,0:T(8,128)(2,1)} async-done(((bf16[1024,4096]{1,0:T(8,128)(2,1)}), bf16[128,4096]{1,0:T(8,128)(2,1)}) %reduce-scatter.12.cloned.1.call-update) | async-done | bytes 1048592 | tf_op jit(solution)/shard_map/reduce_scatter | solution.py:127
  1023.5 35.6 %all-reduce = f32[8,1536]{1,0:T(8,128)S(1)} all-reduce(f32[8,1536]{1,0:T(8,128)S(1)} %constant_dynamic-update-slice_fusion), channel_id=6, replica_groups=mesh['ctx'=4,'fsdp'=8] {'fsdp'}, use_global_device_ids=true, to_apply=%region_25.26.clone | all-reduce | flops 12288 | bytes 98304
  1059.8 6.0 psum.37
  1067.0 5.9 convolution_add_fusion.2
  1072.9 21.8 %all-reduce.4.cloned.1.call-done = (bf16[128,3072]{0,1:T(8,128)(2,1)}, bf16[128,1024]{1,0:T(8,128)(2,1)}, bf16[128,4096]{1,0:T(8,128)(2,1)}, bf16[512,1024]{1,0:T(8,128)(2,1)}) async-done(((bf16[128,3072]{0,1:T(8,128)(2,1)}, bf16[128,1024]{1,0:T(8,128)(2,1)}, bf16[128,4096]{1,0:T(8,128)(2,1)}, bf16[512,1024]{1,0:T(8,128)(2,1)}), (bf16[128,3072]{0,1:T(8,128)(2,1)}, bf16[128,1024]{1,0:T(8,128)(2,1)}, ...) | async-done | bytes 3145744 | tf_op jit(solution)/shard_map/psum | solution.py:128
  (174 shorter events, 102.9 us)
Async XLA Ops:
  7.3 5.9 copy-start.28
  7.3 6.1 copy-start.29
  7.3 105.8 %copy-start.17 = (bf16[2,1,128,1024]{3,2,1,0:T(8,128)(2,1)S(1)}, bf16[2,1,128,1024]{3,2,1,0:T(8,128)(2,1)}, u32[]{:S(2)}) copy-start(bf16[2,1,128,1024]{3,2,1,0:T(8,128)(2,1)} %param.18) | copy-start | bytes 1572868
  7.3 105.8 %all-gather.7.cloned.1.call-start = ((), (), s32[]{:S(2)}) async-start(), calls=%async_computation.5 | async-start | bytes 7077888 | tf_op jit(solution)/shard_map/all_gather | solution.py:123
  9.5 190.3 %all-gather.9.cloned.1.call-start = ((), (), s32[]{:S(2)}) async-start(), calls=%async_computation.6 | async-start | bytes 2359296 | tf_op jit(solution)/shard_map/all_gather | solution.py:123
  10.2 278.1 %all-gather.11.cloned.1.call-start = ((), (), s32[]{:S(2)}) async-start(), calls=%async_computation.7 | async-start | bytes 9437184 | tf_op jit(solution)/shard_map/all_gather | solution.py:123
  11.0 402.4 %all-gather.13.cloned.1.call-start = ((), (), s32[]{:S(2)}) async-start(), calls=%async_computation.8 | async-start | bytes 9437184 | tf_op jit(solution)/shard_map/all_gather | solution.py:123
  11.6 503.9 %reduce-scatter.8.cloned.1.call-start = ((), (), s32[]{:S(2)}) async-start(), calls=%async_computation.9 | async-start | bytes 5242880 | tf_op jit(solution)/shard_map/reduce_scatter | solution.py:233
  119.7 2.9 collective-permute-start
  119.8 7.6 copy-start.20
  119.8 7.7 copy-start.8
  125.9 48.0 %collective-permute-start.1 = (bf16[2,2,128,2048]{3,2,0,1:T(8,128)(2,1)}, bf16[2,2,128,2048]{3,2,0,1:T(8,128)(2,1)}, u32[]{:S(2)}, u32[]{:S(2)}) collective-permute-start(bf16[2,2,128,2048]{3,2,0,1:T(8,128)(2,1)} %pad_maximum_fusion.2), channel_id=1, source_target_pairs={{0,16},{8,24},{16,0},{24,8},{1,17},{9,25},{17,1},{25,9},{2,18},{10... | collective-permute-start | bytes 6291464 | tf_op jit(solution)/shard_map/ppermute | solution.py:22
  413.3 6.8 copy-start.9
  422.0 11.4 %copy-start.12 = (f32[256,1024]{1,0:T(8,128)}, f32[256,1024]{1,0:T(8,128)S(1)}, u32[]{:S(2)}) copy-start(f32[256,1024]{1,0:T(8,128)S(1)} %get-tuple-element.81) | copy-start | bytes 3145732
  433.4 6.9 copy-start.13
  433.4 8.3 copy-start.5
  453.2 6.2 copy-start.15
  472.6 175.5 %reduce-scatter.16.cloned.1.call-start = ((), (), s32[]{:S(2)}) async-start(), calls=%async_computation.13 | async-start | bytes 7077888
  529.9 189.7 %reduce-scatter.10.cloned.1.call-start = ((), (), s32[]{:S(2)}) async-start(), calls=%async_computation.10 | async-start | bytes 2359296 | tf_op jit(solution)/shard_map/reduce_scatter | solution.py:127
  533.3 338.4 %reduce-scatter.14.cloned.1.call-start = ((), (), s32[]{:S(2)}) async-start(), calls=%async_computation.12 | async-start | bytes 9437184 | tf_op jit(solution)/shard_map/reduce_scatter | solution.py:127
  540.9 482.6 %reduce-scatter.12.cloned.1.call-start = ((), (), s32[]{:S(2)}) async-start(), calls=%async_computation.11 | async-start | bytes 9437184 | tf_op jit(solution)/shard_map/reduce_scatter | solution.py:127
  548.3 546.4 %all-reduce.4.cloned.1.call-start = ((), (), s32[]{:S(2)}) async-start(), calls=%async_computation.14 | async-start | bytes 6291456 | tf_op jit(solution)/shard_map/psum | solution.py:128
  1094.7 7.1 copy-start.16
  1097.0 6.3 copy-start.18
  (20 other events, 60.5 us)
Sparse Core Ops, SparseCore 0:
  10.9 102.1 all-gather.6
  115.2 47.4 all-gather.8
  164.8 123.4 all-gather.10
  290.3 123.0 all-gather.12
  472.7 42.7 reduce-scatter.7
  530.1 117.9 reduce-scatter.15
  652.6 67.0 reduce-scatter.9
  723.7 148.0 reduce-scatter.13
  875.4 148.0 reduce-scatter.11
  1026.7 67.9 all-reduce.3
